TPU v7x, 128 devices: a whole 4x4x4 slice. The times are simulated.
128 devices in a mesh: row: 32 (over y, z, core), col: 4 (over x).
Axes of the slice: x: 4, y: 4, z: 4, core: 2. Of those that a mesh axis runs over, the one named last changes fastest.
Arguments:
- amplitudes: bfloat16 [4, 1280, 1280], P(None, ('row', 'col')), may hold values from -0.75 to 0.75
- integrals: bfloat16 [96, 1280, 1280], P('row', 'col'), may hold values from -0.15625 to 0.15625
- occupied_integrals: bfloat16 [96, 160, 1280], P('row'), may hold values from -1 to 1
- pair_orbitals: int32 [4, 2], replicated, may hold values from 0 to 159
- amplitude_tiles: int32 [4, 20, 20], replicated, may hold values 0 or 1
- integral_tiles: int32 [20, 20], replicated, may hold values 0 or 1
Outputs:
- residual: float32 [4, 1280, 1280], P(None, 'col', 'row')
All inputs are finite; a program needn't handle non-finite values.
Results may differ from a plain program's by a relative error of at most 0.005.
Values may be sent and summed in bfloat16 or wider, within the bound.
A program may use at most 128 MiB of HBM per device.

v0:
```python
import jax
import jax.numpy as jnp
from jax import lax
from jax.sharding import PartitionSpec as P

TILE = 64


def mask_rows(amp_rows, amp_tiles, tile_size):
    row_count = amp_rows.shape[1]
    tile_count = amp_tiles.shape[1]
    tile_of = jnp.arange(row_count, dtype=jnp.int32) // tile_size
    picker = (tile_of[:, None] == jnp.arange(tile_count, dtype=jnp.int32)[None, :]).astype(
        jnp.float32
    )
    row_mask = jnp.einsum("nk,pkm->pnm", picker, amp_tiles.astype(jnp.float32))
    row_mask = jnp.repeat(row_mask, tile_size, axis=2)
    return amp_rows * row_mask.astype(amp_rows.dtype)


def local(
    amplitudes, integrals, occupied_integrals, pair_orbitals, amplitude_tiles, integral_tiles
):
    column_index = lax.axis_index("col")
    local_rows = integrals.shape[1]
    tiles_here = local_rows // TILE
    tile_rows = lax.dynamic_slice_in_dim(integral_tiles, column_index * tiles_here, tiles_here, 0)
    factor_mask = jnp.repeat(jnp.repeat(tile_rows, TILE, axis=0), TILE, axis=1)
    masked_int = integrals * factor_mask.astype(jnp.bfloat16)[None]
    orbital_ids = jnp.arange(occupied_integrals.shape[1], dtype=jnp.int32)
    pick_first = (pair_orbitals[:, 0][:, None] == orbital_ids[None, :]).astype(jnp.bfloat16)
    pick_second = (pair_orbitals[:, 1][:, None] == orbital_ids[None, :]).astype(jnp.bfloat16)
    first_rows = jnp.einsum(
        "po,qov->qpv", pick_first, occupied_integrals, preferred_element_type=jnp.float32
    )
    second_rows = jnp.einsum(
        "po,qov->qpv", pick_second, occupied_integrals, preferred_element_type=jnp.float32
    ).astype(jnp.bfloat16)
    whole_amp = lax.all_gather(amplitudes, ("row", "col"), axis=1, tiled=True)
    masked_amp = mask_rows(whole_amp, amplitude_tiles, TILE)
    inter = jnp.einsum(
        "qac,pcd->qpad", masked_int, masked_amp, preferred_element_type=jnp.float32
    ).astype(jnp.bfloat16)
    carried = jnp.einsum(
        "qpc,pcd->qpd", second_rows, masked_amp, preferred_element_type=jnp.float32
    )
    first_here = lax.dynamic_slice_in_dim(first_rows, column_index * local_rows, local_rows, 2)
    ladder = jnp.einsum(
        "qpad,qbd->pab",
        inter,
        lax.all_gather(masked_int, "col", axis=1, tiled=True),
        preferred_element_type=jnp.float32,
    )
    cycle = jnp.einsum("qpa,qpb->pab", first_here, carried)
    return lax.psum_scatter(ladder + cycle, "row", scatter_dimension=2, tiled=True)


def solution(mesh):
    placed = (
        P(None, ("row", "col"), None),
        P("row", "col", None),
        P("row", None, None),
        P(),
        P(),
        P(),
    )
    return jax.shard_map(
        local, mesh=mesh, in_specs=placed, out_specs=P(None, "col", "row"), check_vma=False
    )
```

profile of v0, /device:TPU:0, one launch (start us, length us, event | category | flops | bytes accessed | tf_op | source)
XLA Modules:
  0.0 317.9 jit_solution(4331648339381374294)
XLA Ops:
  6.5 0.0 copy-start
  6.5 0.0 copy-start.4
  6.5 0.0 copy-start.5
  6.5 0.0 all-gather.3.cloned.1.call-start
  6.5 0.7 all-gather.3.cloned.1.call-update
  7.3 0.0 all-gather.5.cloned.1.call-start
  7.3 0.7 dynamic-slice_convert_fusion
  8.0 0.1 copy.23
  8.1 0.1 broadcast_in_dim.7
  8.2 0.1 convert_element_type.48
  8.3 0.1 broadcast_in_dim.16
  8.4 0.6 copy.24
  9.0 3.4 %broadcast_multiply_fusion = bf16[3,320,1280]{2,1,0:T(8,128)(2,1)} fusion(bf16[3,320,1280]{2,1,0:T(8,128)(2,1)} %param.7, bf16[320,1280]{1,0:T(8,128)(2,1)S(1)} %copy.24), kind=kLoop, calls=%fused_computation.13 | loop fusion | flops 1228800 | bytes 5734400 | tf_op jit(solution)/shard_map/mul | solution.py:29
  12.5 0.0 all-gather.5.cloned.1.call-update
  12.5 0.0 reduce-scatter.2.cloned.1.call-start
  12.6 0.0 copy-done.4
  12.6 0.0 copy-done.5
  12.6 0.0 copy-done
  12.6 0.3 fusion.20
  12.9 0.1 dynamic-slice_bitcast_fusion
  13.0 0.3 fusion.7
  13.3 0.3 fusion.8
  13.6 73.3 %all-gather.3.cloned.1.call-done = bf16[4,1280,1280]{2,0,1:T(4,128)(2,1)} async-done(((bf16[4,10,1280]{2,0,1:T(4,128)(2,1)}), bf16[4,1280,1280]{2,0,1:T(4,128)(2,1)}) %all-gather.3.cloned.1.call-update) | async-done | bytes 13107216 | tf_op jit(solution)/shard_map/all_gather | solution.py:39
  87.0 21.2 %copy.22 = bf16[4,1280,1280]{1,2,0:T(8,128)(2,1)} copy(bf16[4,1280,1280]{2,0,1:T(4,128)(2,1)} %all-gather.3.cloned.1.call-done) | data formatting | bytes 26214400 | tf_op jit(solution)/shard_map/all_gather | solution.py:39
  108.2 0.0 copy-start.3
  108.2 6.3 %bitcast_multiply_fusion = bf16[4,1280,1280]{1,2,0:T(8,128)(2,1)S(1)} fusion(bf16[4,1280,1280]{1,2,0:T(8,128)(2,1)} %copy.22, bf16[4,1280,20]{1,2,0:T(8,128)(2,1)S(1)} %fusion.7), kind=kLoop, calls=%fused_computation.2 | loop fusion | flops 6553600 | bytes 26419200 | tf_op jit(solution)/shard_map/mul | solution.py:18
  114.6 0.0 copy-start.2
  114.6 4.7 %copy-done.2 = bf16[4,1280,1280]{1,2,0:T(8,128)(2,1)} copy-done((bf16[4,1280,1280]{1,2,0:T(8,128)(2,1)}, bf16[4,1280,1280]{1,2,0:T(8,128)(2,1)S(1)}, u32[]{:S(2)}) %copy-start.2) | copy-done | bytes 13107224
  119.3 0.0 copy-done.3
  119.3 15.0 %fusion.1 = bf16[3,4,320,1280]{3,2,0,1:T(8,128)(2,1)} fusion(bf16[4,1280,1280]{1,2,0:T(8,128)(2,1)S(1)} %bitcast_multiply_fusion, bf16[3,320,1280]{2,1,0:T(8,128)(2,1)S(1)} %copy-done.3), kind=kOutput, calls=%fused_computation.3 | convolution fusion | flops 12587827200 | bytes 25395200 | tf_op jit(solution)/shard_map/qac,pcd->qpad/dot_general | solution.py:41
  134.3 49.2 %all-gather.5.cloned.1.call-done = bf16[3,1280,1280]{2,1,0:T(8,128)(2,1)} async-done(((bf16[3,320,1280]{2,1,0:T(8,128)(2,1)}), bf16[3,1280,1280]{2,1,0:T(8,128)(2,1)}) %all-gather.5.cloned.1.call-update) | async-done | bytes 9830416 | tf_op jit(solution)/shard_map/all_gather | solution.py:51
  183.4 21.9 %fusion.4 = f32[4,320,1280,1]{1,2,3,0:T(8,128)} fusion(bf16[3,4,320,1280]{3,2,0,1:T(8,128)(2,1)} %fusion.1, bf16[3,1280,1280]{2,1,0:T(8,128)(2,1)} %all-gather.5.cloned.1.call-done), kind=kOutput, calls=%fused_computation.4 | convolution fusion | flops 12582912000 | bytes 26214400 | tf_op jit(solution)/shard_map/qpad,qbd->pab/dot_general | solution.py:48
  205.3 0.0 copy-start.1
  205.3 14.8 %bitcast_add_fusion = f32[4,320,1280]{1,2,0:T(8,128)} fusion(f32[4,320,1280,1]{1,2,3,0:T(8,128)} %fusion.4, bf16[4,1280,1280]{1,2,0:T(8,128)(2,1)} %copy-done.2, bf16[3,4,1280]{2,1,0:T(4,128)(2,1)S(1)} %fusion.8, bf16[3,4,320]{2,1,0:T(4,128)(2,1)S(1)} %dynamic-slice_bitcast_fusion), kind=kOutput, calls=%fused_computation.6 | convolution fusion | flops 50790400 | bytes 26252800 | tf_op jit(solution)/shard_map/qpa,qpb->pab/dot_general | solution.py:54
  220.1 0.0 reduce-scatter.2.cloned.1.call-update
  220.1 91.3 %reduce-scatter.2.cloned.1.call-done = f32[4,320,40]{1,2,0:T(8,128)} async-done(((f32[4,320,1280]{1,2,0:T(8,128)}), f32[4,320,40]{1,2,0:T(8,128)}) %reduce-scatter.2.cloned.1.call-update) | async-done | bytes 204816 | tf_op jit(solution)/shard_map/reduce_scatter | solution.py:55
  311.4 0.0 copy-done.1
  (3 shorter events, 0.0 us)
Async XLA Ops:
  6.5 6.1 %copy-start = (bf16[3,160,1280]{2,1,0:T(8,128)(2,1)S(1)}, bf16[3,160,1280]{2,1,0:T(8,128)(2,1)}, u32[]{:S(2)}) copy-start(bf16[3,160,1280]{2,1,0:T(8,128)(2,1)} %param.8) | copy-start | bytes 3686404
  6.5 6.0 %copy-start.4 = (s32[4,20,20]{2,0,1:T(4,128)S(1)}, s32[4,20,20]{2,0,1:T(4,128)}, u32[]{:S(2)}) copy-start(s32[4,20,20]{2,0,1:T(4,128)} %param.10) | copy-start | bytes 19204
  6.5 6.1 %copy-start.5 = (s32[4,2]{0,1:T(2,128)S(1)}, s32[4,2]{0,1:T(2,128)}, u32[]{:S(2)}) copy-start(s32[4,2]{0,1:T(2,128)} %param.9) | copy-start | bytes 100
  6.5 80.5 %all-gather.3.cloned.1.call-start = ((), (), s32[]{:S(2)}) async-start(), calls=%async_computation.1 | async-start | bytes 13209600 | tf_op jit(solution)/shard_map/all_gather | solution.py:39
  7.3 176.2 %all-gather.5.cloned.1.call-start = ((), (), s32[]{:S(2)}) async-start(), calls=%async_computation.2 | async-start | bytes 12288000 | tf_op jit(solution)/shard_map/all_gather | solution.py:51
  12.5 298.9 %reduce-scatter.2.cloned.1.call-start = ((), (), s32[]{:S(2)}) async-start(), calls=%async_computation.3 | async-start | bytes 8110080 | tf_op jit(solution)/shard_map/reduce_scatter | solution.py:55
  108.2 11.0 %copy-start.3 = (bf16[3,320,1280]{2,1,0:T(8,128)(2,1)S(1)}, bf16[3,320,1280]{2,1,0:T(8,128)(2,1)}, u32[]{:S(2)}) copy-start(bf16[3,320,1280]{2,1,0:T(8,128)(2,1)} %broadcast_multiply_fusion) | copy-start | bytes 7372804
  114.6 4.7 %copy-start.2 = (bf16[4,1280,1280]{1,2,0:T(8,128)(2,1)}, bf16[4,1280,1280]{1,2,0:T(8,128)(2,1)S(1)}, u32[]{:S(2)}) copy-start(bf16[4,1280,1280]{1,2,0:T(8,128)(2,1)S(1)} %bitcast_multiply_fusion) | copy-start | bytes 39321604
  205.3 106.1 %copy-start.1 = (bf16[3,160,1280]{2,1,0:T(8,128)(2,1)S(1)}, bf16[3,160,1280]{2,1,0:T(8,128)(2,1)}, u32[]{:S(2)}) copy-start(bf16[3,160,1280]{2,1,0:T(8,128)(2,1)} %param.8) | copy-start | bytes 3686404
Sparse Core Ops, SparseCore 0:
  10.3 76.6 all-gather.2
  88.7 94.7 all-gather.4
  220.2 91.0 reduce-scatter.1
where the time goes:
time: 319 us; the launch traced here: 318 us
  waiting for transfers between devices  215 us (67%)
  matrix products  52.6 us (16%)
  local copies, waits for them, and re-layouts  27 us (8%)
  between operations  13.2 us (4%)
  other arithmetic  10.5 us (3%)
    reduce_scatter x1, waiting for transfers between devices, local(): lax.psum_scatter(ladder + cycle, 'row', scatter_dimension=2, tiled=True)  91.3 us
    all_gather x1, waiting for transfers between devices, local(): whole_amp = lax.all_gather(amplitudes, ('row', 'col'), axis=1, tiled=True)  73.3 us
    all_gather x1, waiting for transfers between devices, local(): lax.all_gather(masked_int, 'col', axis=1, tiled=True)  49.2 us
    dot_general x1, matrix products, local(): jnp.einsum('qpad,qbd->pab', inter, lax.all_gather(masked_int, 'col', axis...  21.9 us
    all_gather x1, local copies, waits for them, and re-layouts, local(): whole_amp = lax.all_gather(amplitudes, ('row', 'col'), axis=1, tiled=True)  21.2 us
    dot_general x1, matrix products, local(): jnp.einsum('qac,pcd->qpad', masked_int, masked_amp, preferred_element_typ...  15 us
    dot_general x1, matrix products, local(): cycle = jnp.einsum('qpa,qpb->pab', first_here, carried)  14.8 us
  transfers between devices with their start and end apart: 3, of which 3 were waited for; matrix products, arithmetic and copies ran while one was open for 15% of the time, Pallas kernels for 0%

commit v1 on v0

--- a/solution.py
+++ b/solution.py
@@ -4,6 +4,13 @@
 from jax.sharding import PartitionSpec as P
 
 TILE = 64
+
+
+def exchange_gather(x, axis, dim):
+    size = lax.axis_size(axis)
+    blocks = jnp.stack([x for _ in range(size)])
+    blocks = lax.all_to_all(blocks, axis, split_axis=0, concat_axis=0)
+    return jnp.concatenate(blocks, axis=dim)
 
 
 def mask_rows(amp_rows, amp_tiles, tile_size):
@@ -48,7 +55,7 @@
     ladder = jnp.einsum(
         "qpad,qbd->pab",
         inter,
-        lax.all_gather(masked_int, "col", axis=1, tiled=True),
+        exchange_gather(masked_int, "col", 1),
         preferred_element_type=jnp.float32,
     )
     cycle = jnp.einsum("qpa,qpb->pab", first_here, carried)

time: 319 us -> 341 us (1.069)
  local copies, waits for them, and re-layouts: 27 us -> 36.3 us
  waiting for transfers between devices: 215 us -> 222 us
  starting transfers between devices: 0.08 us -> 6.1 us
    all_to_all x0 -> x1, waiting for transfers between devices: none -> 131 us  [exchange_gather(): blocks = lax.all_to_all(blocks, axis, split_axis=0, concat_axis=0)]
    all_gather x1, waiting for transfers between devices: 73.3 us -> 0.01 us  [local(): whole_amp = lax.all_gather(amplitudes, ('row', 'col'), axis=1, tiled=True)]
    all_gather x1 -> x0, waiting for transfers between devices: 49.2 us -> none  [local(): lax.all_gather(masked_int, 'col', axis=1, tiled=True)]
    reshape x0 -> x1, local copies, waits for them, and re-layouts: none -> 8.22 us  [exchange_gather(): return jnp.concatenate(blocks, axis=dim)]
    all_to_all x0 -> x1, starting transfers between devices: none -> 6.06 us  [exchange_gather(): blocks = lax.all_to_all(blocks, axis, split_axis=0, concat_axis=0)]
    another operation x0 -> x1, local copies, waits for them, and re-layouts: none -> 4.69 us  [exchange_gather(): blocks = jnp.stack([x for _ in range(size)])]
  transfers between devices with their start and end apart: 3 -> 3, of which waited for: 3 -> 2; matrix products, arithmetic and copies ran while one was open for 15% -> 5% of each run, Pallas kernels for 0% -> 0%
where the time goes in v1:
time: 341 us; the launch traced here: 340 us
  waiting for transfers between devices  222 us (65%)
  matrix products  52.6 us (15%)
  local copies, waits for them, and re-layouts  36.3 us (11%)
  between operations  13.5 us (4%)
  other arithmetic  8.95 us (3%)
  starting transfers between devices  6.1 us (2%)
    all_to_all x1, waiting for transfers between devices, exchange_gather(): blocks = lax.all_to_all(blocks, axis, split_axis=0, concat_axis=0)  131 us
    reduce_scatter x1, waiting for transfers between devices, local(): lax.psum_scatter(ladder + cycle, 'row', scatter_dimension=2, tiled=True)  90.7 us
    dot_general x1, matrix products, local(): jnp.einsum('qpad,qbd->pab', inter, exchange_gather(masked_int, 'col', 1),...  21.9 us
    all_gather x1, local copies, waits for them, and re-layouts, local(): whole_amp = lax.all_gather(amplitudes, ('row', 'col'), axis=1, tiled=True)  20.9 us
    dot_general x1, matrix products, local(): jnp.einsum('qac,pcd->qpad', masked_int, masked_amp, preferred_element_typ...  15 us
    dot_general x1, matrix products, local(): cycle = jnp.einsum('qpa,qpb->pab', first_here, carried)  14.8 us
    reshape x1, local copies, waits for them, and re-layouts, exchange_gather(): return jnp.concatenate(blocks, axis=dim)  8.22 us
  transfers between devices with their start and end apart: 3, of which 2 were waited for; matrix products, arithmetic and copies ran while one was open for 5% of the time, Pallas kernels for 0%

profile of v1, /device:TPU:0, one launch (start us, length us, event | category | flops | bytes accessed | tf_op | source)
XLA Modules:
  0.0 340.0 jit_solution(11305332592900037119)
XLA Ops:
  6.5 0.0 copy-start
  6.5 0.0 all-gather.2.cloned.1.call-start
  6.5 0.7 all-gather.2.cloned.1.call-update
  7.3 0.7 dynamic-slice_convert_fusion
  8.0 0.1 copy.23
  8.1 0.1 broadcast_in_dim.7
  8.2 0.1 convert_element_type.48
  8.3 0.1 broadcast_in_dim.16
  8.4 0.6 copy.24
  9.0 1.9 broadcast_multiply_fusion
  10.9 0.0 copy-start.3
  10.9 1.4 copy-done.3
  12.3 4.7 %stack.2 = bf16[4,3,320,1280]{3,2,1,0:T(8,128)(2,1)} broadcast(bf16[3,320,1280]{2,1,0:T(8,128)(2,1)S(1)} %broadcast_multiply_fusion), dimensions={1,2,3} | broadcast | bytes 12288000 | tf_op jit(solution)/shard_map/stack | solution.py:11
  17.0 0.0 copy-start.5
  17.0 0.0 copy-start.6
  17.0 6.1 %all-to-all-start = ((bf16[4,3,320,1280]{3,2,1,0:T(8,128)(2,1)}), bf16[4,3,320,1280]{3,2,1,0:T(8,128)(2,1)}, u32[]{:S(2)}, u32[]{:S(2)}) async-start(bf16[4,3,320,1280]{3,2,1,0:T(8,128)(2,1)} %stack.2), calls=%async_computation | async-start | bytes 19660800 | tf_op jit(solution)/shard_map/all_to_all | solution.py:12
  23.1 0.0 reduce-scatter.2.cloned.1.call-start
  23.1 0.0 copy-done.5
  23.2 0.0 copy-done.6
  23.2 0.0 copy-done
  23.2 0.3 fusion.23
  23.5 0.1 dynamic-slice_bitcast_fusion
  23.6 0.3 fusion.10
  23.9 0.3 fusion.11
  24.2 131.1 %all-to-all-done = bf16[4,3,320,1280]{3,2,1,0:T(8,128)(2,1)} async-done(((bf16[4,3,320,1280]{3,2,1,0:T(8,128)(2,1)}), bf16[4,3,320,1280]{3,2,1,0:T(8,128)(2,1)}, u32[]{:S(2)}, u32[]{:S(2)}) %all-to-all-start) | async-done | bytes 9830432 | tf_op jit(solution)/shard_map/all_to_all | solution.py:12
  155.3 8.2 %copy.26 = bf16[3,4,320,1280]{3,2,1,0:T(8,128)(2,1)} copy(bf16[3,4,320,1280]{3,2,0,1:T(8,128)(2,1)} %bitcast.7) | data formatting | bytes 19660800 | tf_op jit(solution)/shard_map/reshape | solution.py:13
  163.5 0.0 all-gather.2.cloned.1.call-done
  163.5 20.9 %copy.22 = bf16[4,1280,1280]{1,2,0:T(8,128)(2,1)} copy(bf16[4,1280,1280]{2,0,1:T(4,128)(2,1)} %all-gather.2.cloned.1.call-done) | data formatting | bytes 26214400 | tf_op jit(solution)/shard_map/all_gather | solution.py:46
  184.4 0.0 copy-start.4
  184.4 6.3 %bitcast_multiply_fusion = bf16[4,1280,1280]{1,2,0:T(8,128)(2,1)S(1)} fusion(bf16[4,1280,1280]{1,2,0:T(8,128)(2,1)} %copy.22, bf16[4,1280,20]{1,2,0:T(8,128)(2,1)S(1)} %fusion.10), kind=kLoop, calls=%fused_computation.2 | loop fusion | flops 6553600 | bytes 26419200 | tf_op jit(solution)/shard_map/mul | solution.py:25
  190.7 0.0 copy-done.4
  190.7 0.0 copy-start.2
  190.7 15.0 %fusion.1.clone.4 = bf16[3,4,320,1280]{3,2,0,1:T(8,128)(2,1)} fusion(bf16[4,1280,1280]{1,2,0:T(8,128)(2,1)S(1)} %bitcast_multiply_fusion, bf16[3,320,1280]{2,1,0:T(8,128)(2,1)S(1)} %copy-done.4), kind=kOutput, calls=%fused_computation.3.clone.clone.clone.1 | convolution fusion | flops 12587827200 | bytes 25395200 | tf_op jit(solution)/shard_map/qac,pcd->qpad/dot_general | solution.py:48
  205.7 0.0 copy-done.2
  205.7 21.9 %fusion.7 = f32[4,320,1280,1]{1,2,3,0:T(8,128)} fusion(bf16[3,1280,1280,1]{2,1,0,3:T(8,128)(2,1)} %bitcast.68, bf16[3,4,320,1280]{3,2,0,1:T(8,128)(2,1)} %fusion.1.clone.4), kind=kOutput, calls=%fused_computation.7 | convolution fusion | flops 12582912000 | bytes 26214400 | tf_op jit(solution)/shard_map/qpad,qbd->pab/dot_general | solution.py:55
  227.6 0.0 copy-start.1
  227.6 14.8 %bitcast_add_fusion = f32[4,320,1280]{1,2,0:T(8,128)} fusion(f32[4,320,1280,1]{1,2,3,0:T(8,128)} %fusion.7, bf16[4,1280,1280]{1,2,0:T(8,128)(2,1)} %copy-done.2, bf16[3,4,1280]{2,1,0:T(4,128)(2,1)S(1)} %fusion.11, bf16[3,4,320]{2,1,0:T(4,128)(2,1)S(1)} %dynamic-slice_bitcast_fusion), kind=kOutput, calls=%fused_computation.4 | convolution fusion | flops 50790400 | bytes 26252800 | tf_op jit(solution)/shard_map/qpa,qpb->pab/dot_general | solution.py:61
  242.4 0.0 reduce-scatter.2.cloned.1.call-update
  242.4 90.7 %reduce-scatter.2.cloned.1.call-done = f32[4,320,40]{1,2,0:T(8,128)} async-done(((f32[4,320,1280]{1,2,0:T(8,128)}), f32[4,320,40]{1,2,0:T(8,128)}) %reduce-scatter.2.cloned.1.call-update) | async-done | bytes 204816 | tf_op jit(solution)/shard_map/reduce_scatter | solution.py:62
  333.1 0.0 copy-done.1
  (3 shorter events, 0.0 us)
Async XLA Ops:
  6.5 16.7 %copy-start = (bf16[3,160,1280]{2,1,0:T(8,128)(2,1)S(1)}, bf16[3,160,1280]{2,1,0:T(8,128)(2,1)}, u32[]{:S(2)}) copy-start(bf16[3,160,1280]{2,1,0:T(8,128)(2,1)} %param.8) | copy-start | bytes 3686404
  6.5 157.0 %all-gather.2.cloned.1.call-start = ((), (), s32[]{:S(2)}) async-start(), calls=%async_computation.2 | async-start | bytes 13209600 | tf_op jit(solution)/shard_map/all_gather | solution.py:46
  10.9 1.4 copy-start.3
  17.0 6.1 %copy-start.5 = (s32[4,20,20]{2,0,1:T(4,128)S(1)}, s32[4,20,20]{2,0,1:T(4,128)}, u32[]{:S(2)}) copy-start(s32[4,20,20]{2,0,1:T(4,128)} %param.10) | copy-start | bytes 19204
  17.0 6.2 %copy-start.6 = (s32[4,2]{0,1:T(2,128)S(1)}, s32[4,2]{0,1:T(2,128)}, u32[]{:S(2)}) copy-start(s32[4,2]{0,1:T(2,128)} %param.9) | copy-start | bytes 100
  17.0 138.3 %all-to-all-start = ((bf16[4,3,320,1280]{3,2,1,0:T(8,128)(2,1)}), bf16[4,3,320,1280]{3,2,1,0:T(8,128)(2,1)}, u32[]{:S(2)}, u32[]{:S(2)}) async-start(bf16[4,3,320,1280]{3,2,1,0:T(8,128)(2,1)} %stack.2), calls=%async_computation | async-start | bytes 19660800 | tf_op jit(solution)/shard_map/all_to_all | solution.py:12
  23.1 310.0 %reduce-scatter.2.cloned.1.call-start = ((), (), s32[]{:S(2)}) async-start(), calls=%async_computation.3 | async-start | bytes 8110080 | tf_op jit(solution)/shard_map/reduce_scatter | solution.py:62
  184.4 6.3 %copy-start.4 = (bf16[3,320,1280]{2,1,0:T(8,128)(2,1)S(1)}, bf16[3,320,1280]{2,1,0:T(8,128)(2,1)}, u32[]{:S(2)}) copy-start(bf16[3,320,1280]{2,1,0:T(8,128)(2,1)} %copy-done.3) | copy-start | bytes 7372804
  190.7 15.0 %copy-start.2 = (bf16[4,1280,1280]{1,2,0:T(8,128)(2,1)}, bf16[4,1280,1280]{1,2,0:T(8,128)(2,1)S(1)}, u32[]{:S(2)}) copy-start(bf16[4,1280,1280]{1,2,0:T(8,128)(2,1)S(1)} %bitcast_multiply_fusion) | copy-start | bytes 39321604
  227.6 105.5 %copy-start.1 = (bf16[3,160,1280]{2,1,0:T(8,128)(2,1)S(1)}, bf16[3,160,1280]{2,1,0:T(8,128)(2,1)}, u32[]{:S(2)}) copy-start(bf16[3,160,1280]{2,1,0:T(8,128)(2,1)} %param.8) | copy-start | bytes 3686404
Sparse Core Ops, SparseCore 0:
  10.3 95.2 all-gather.1
  242.6 90.5 reduce-scatter.1
